TPU v7x, 32 devices: a whole 2x2x4 slice. The times are simulated.
32 devices in a mesh: tm: 2 (over y), height: 16 (over z, x, core).
Axes of the slice: x: 2, y: 2, z: 4, core: 2. Of those that a mesh axis runs over, the one named last changes fastest.
Arguments:
- activations: bfloat16 [4, 64, 256, 128], P('tm', 'height'), may hold values from -60 to 60
- norm_gain: float32 [128], replicated, may hold values from 0.1 to 1.9
- norm_bias: float32 [128], replicated, may hold values from -3 to 3
- conv_weight: bfloat16 [3456, 256], replicated, may hold values from -0.109375 to 0.109375
- cotangent: bfloat16 [2, 64, 256, 256], P('tm', 'height'), may hold values from -6 to 6
Outputs:
- pooled: bfloat16 [2, 64, 256, 256], P('tm', None, 'height')
- weight_grad: bfloat16 [256, 3456], P('height')
All inputs are finite; a program needn't handle non-finite values.
Results may differ from a plain program's by a relative error of at most 0.0056.
Values may be sent and summed in bfloat16 or wider, within the bound.
A program may use at most 128 MiB of HBM per device.

v0:
```python
import math

import jax
import jax.numpy as jnp
from jax import lax
from jax.sharding import PartitionSpec as P

GROUPS = 32
KT = 3


def shifted(value, axis, steps):
    count = lax.axis_size(axis)
    first, last = (max(0, -steps), min(count, count - steps))
    return lax.ppermute(value, axis, [(source, source + steps) for source in range(first, last)])


def extended(cells, sides, width):
    for axis, dim in sides:
        count = lax.axis_size(axis)
        ends = count - 1
        head = lax.slice_in_dim(cells, 0, width, axis=dim)
        tail = lax.slice_in_dim(cells, cells.shape[dim] - width, cells.shape[dim], axis=dim)
        cells = jnp.concatenate(
            [
                lax.ppermute(tail, axis, [(i, (i + 1) % count) for i in range(ends)]),
                cells,
                lax.ppermute(head, axis, [((i + 1) % count, i) for i in range(ends)]),
            ],
            axis=dim,
        )
    return cells


def pool_pairs(values):
    paired = values.reshape((values.shape[0] // 2, 2) + values.shape[1:])
    return ((paired[:, 0].astype(jnp.float32) + paired[:, 1].astype(jnp.float32)) * 0.5).astype(
        jnp.bfloat16
    )


def local(activations, norm_gain, norm_bias, conv_weight, cotangent):
    frames, rows, width, channels = activations.shape
    n_out = conv_weight.shape[1]
    per_group = channels // GROUPS
    n_time = lax.axis_size("tm")
    n_rows = lax.axis_size("height")
    entries = frames * rows * width * per_group * n_time * n_rows
    grouped = activations.reshape(frames * rows * width, GROUPS, per_group)
    local_sums = jnp.sum(grouped, axis=(0, 2), dtype=jnp.float32)
    group_mean = lax.psum(local_sums, ("tm", "height")) / entries
    centered = grouped.astype(jnp.float32) - group_mean[None, :, None]
    group_var = lax.psum(jnp.sum(centered * centered, axis=(0, 2)), ("tm", "height")) / entries
    mean_chan = jnp.repeat(group_mean, per_group)
    inv_chan = jnp.repeat(lax.rsqrt(group_var + 1e-06), per_group)
    normed = jax.nn.silu(
        (activations.astype(jnp.float32) - mean_chan) * inv_chan * norm_gain + norm_bias
    ).astype(jnp.bfloat16)
    earlier = shifted(normed, "tm", 1)
    first_frame = jnp.broadcast_to(normed[:1], earlier.shape)
    earlier = jnp.where(lax.axis_index("tm") == 0, first_frame, earlier)
    stacked = jnp.concatenate([earlier, normed], axis=0)
    padded = extended(stacked, (("height", 1),), 1)
    padded = jnp.pad(padded, ((0, 0), (0, 0), (1, 1), (0, 0)))
    patches = jnp.concatenate([padded[:, :, tap_c : tap_c + width] for tap_c in range(KT)], axis=3)
    band = KT * channels
    output = jnp.zeros((frames, rows, n_out, width), jnp.float32)
    for tap_t in range(KT):
        for tap_r in range(KT):
            start_row = (tap_t * KT + tap_r) * band
            output = output + jnp.einsum(
                "frwk,kc->frcw",
                patches[tap_t : tap_t + frames, tap_r : tap_r + rows],
                conv_weight[start_row : start_row + band],
                preferred_element_type=jnp.float32,
            )
    conv_out = output.astype(jnp.bfloat16)
    moved = lax.all_to_all(conv_out, "height", split_axis=2, concat_axis=1, tiled=True)
    pooled = pool_pairs(moved)
    upsampled = jnp.repeat(cotangent * jnp.asarray(0.5, jnp.bfloat16), 2, axis=0)
    own_rows = n_out // n_rows
    blocks = []
    for tap_t in range(KT):
        for tap_r in range(KT):
            blocks.append(
                jnp.einsum(
                    "frwk,frwc->ck",
                    patches[tap_t : tap_t + frames, tap_r : tap_r + rows],
                    upsampled,
                    preferred_element_type=jnp.float32,
                )
            )
    summed = lax.psum(jnp.concatenate(blocks, axis=1), ("tm", "height"))
    own_grad = lax.dynamic_slice_in_dim(summed, lax.axis_index("height") * own_rows, own_rows, 0)
    factor = 1.0 / math.sqrt(frames * n_time * rows * n_rows * width)
    weight_grad = (own_grad * factor).astype(jnp.bfloat16)
    return (pooled, weight_grad)


def solution(mesh):
    in_specs = (P("tm", "height", None, None), P(), P(), P(), P("tm", "height", None, None))
    out_specs = (P("tm", None, "height", None), P("height", None))
    return jax.shard_map(local, mesh=mesh, in_specs=in_specs, out_specs=out_specs, check_vma=False)
```

profile of v0, /device:TPU:0, one launch (start us, length us, event | category | flops | bytes accessed | tf_op | source)
XLA Modules:
  0.0 317.6 jit_solution(3643180153994988676)
XLA Ops:
  7.2 0.0 copy-start.2
  7.2 0.0 all-reduce.3.cloned.1.call-start
  7.2 1.4 convert_reduce_fusion
  8.6 0.1 reduce_sum.24
  8.7 0.1 reduce_sum.25
  8.8 42.0 %psum.21 = f32[32]{0:T(128)S(1)} all-reduce(f32[32]{0:T(128)S(1)} %reduce_sum.25), channel_id=1, replica_groups=mesh['tm'=2,'height'=16] {'tm','height'}, use_global_device_ids=true, to_apply=%region_2.0 | all-reduce | flops 32 | bytes 256 | tf_op jit(solution)/shard_map/psum | solution.py:51
  50.9 0.1 broadcast_in_dim.8
  50.9 0.1 sub.7
  51.0 1.3 fusion.79
  52.4 0.1 reduce_sum.36
  52.5 0.1 reduce_sum.37
  52.6 40.2 %psum.22 = f32[32]{0:T(128)S(1)} all-reduce(f32[32]{0:T(128)S(1)} %reduce_sum.37), channel_id=1, replica_groups=mesh['tm'=2,'height'=16] {'tm','height'}, use_global_device_ids=true, to_apply=%region_5.6 | all-reduce | flops 32 | bytes 256 | tf_op jit(solution)/shard_map/psum | solution.py:53
  92.8 0.1 broadcast_in_dim.18
  92.8 0.1 mul.59
  92.9 1.4 fusion.87
  94.4 4.2 %collective-permute-start = (bf16[2,4,256,128]{3,2,1,0:T(8,128)(2,1)S(1)}, bf16[2,4,256,128]{3,2,1,0:T(8,128)(2,1)S(1)}, u32[]{:S(2)}, u32[]{:S(2)}) collective-permute-start(bf16[2,4,256,128]{3,2,1,0:T(8,128)(2,1)S(1)} %fusion.87), channel_id=1, source_target_pairs={{0,16},{1,17},{2,18},{3,19},{4,20},{5,21},{6,22},{7,23},{8,24},{9,... | collective-permute-start | bytes 1572872 | tf_op jit(solution)/shard_map/ppermute | solution.py:15
  98.6 10.2 %collective-permute-done = bf16[2,4,256,128]{3,2,1,0:T(8,128)(2,1)S(1)} collective-permute-done((bf16[2,4,256,128]{3,2,1,0:T(8,128)(2,1)S(1)}, bf16[2,4,256,128]{3,2,1,0:T(8,128)(2,1)S(1)}, u32[]{:S(2)}, u32[]{:S(2)}) %collective-permute-start) | collective-permute-done | bytes 524320 | tf_op jit(solution)/shard_map/ppermute | solution.py:15
  109.0 1.3 collective-permute-start.2
  110.3 3.0 collective-permute-start.1
  113.3 0.0 copy-done.2
  113.4 0.2 copy.17
  113.6 0.0 collective-permute-done.2
  113.6 0.8 collective-permute-done.1
  114.5 0.5 select_maximum_fusion
  114.9 1.1 fusion.124
  116.0 0.0 copy-start.1
  116.0 2.1 pad_maximum_fusion
  118.1 0.0 copy-done.1
  118.1 0.0 copy-start
  118.1 0.7 fusion.99
  118.8 2.2 fusion.101
  121.0 2.0 fusion.103
  123.0 2.0 fusion.105
  125.0 2.0 fusion.107
  127.0 2.1 fusion.109
  129.1 2.1 fusion.113
  131.1 2.1 fusion.111
  133.2 1.5 fusion.28
  134.7 1.5 fusion.34
  136.2 1.5 fusion.40
  137.8 1.5 fusion.46
  139.3 1.5 fusion.52
  140.7 1.5 fusion.58
  142.3 1.6 fusion.64
  143.8 1.5 fusion.70
  145.3 0.0 copy-done
  145.3 1.5 fusion.76
  146.8 0.0 all-reduce.3.cloned.1.call-update
  146.9 6.7 %fusion.22 = bf16[2,4,256,256]{2,3,1,0:T(8,128)(2,1)S(1)} fusion(bf16[4,6,256,384]{3,2,1,0:T(8,128)(2,1)} %copy-done, f32[2,4,256,256]{3,2,1,0:T(8,128)S(1)} %fusion.99, f32[2,4,256,256]{3,2,1,0:T(8,128)} %fusion.101, f32[2,4,256,256]{3,2,1,0:T(8,128)} %fusion.103, f32[2,4,256,256]{3,2,1,0:T(8,128)} %fusion.105, f32[2,4,256,256]{3,2,1,0:T(8,128)} %fusion.107, ...), kind=kOutput, calls=%fused_computation.28 | convolution fusion | flops 407371776 | bytes 22740992 | tf_op jit(solution)/shard_map/frwk,kc->frcw/dot_general | solution.py:71
  153.6 1.8 copy.14
  155.4 8.7 %all-to-all-start = ((bf16[2,4,256,256]{3,1,0,2:T(4,128)(2,1)}), bf16[2,4,256,256]{3,1,0,2:T(4,128)(2,1)S(1)}, u32[]{:S(2)}, u32[]{:S(2)}) async-start(bf16[2,4,256,256]{3,1,0,2:T(4,128)(2,1)} %copy.14), calls=%async_computation | async-start | bytes 2097152 | tf_op jit(solution)/shard_map/all_to_all | solution.py:78
  164.2 143.7 %all-reduce.3.cloned.1.call-done = f32[256,3456]{1,0:T(8,128)} async-done(((f32[256,3456]{1,0:T(8,128)}), f32[256,3456]{1,0:T(8,128)}) %all-reduce.3.cloned.1.call-update) | async-done | bytes 3538960 | tf_op jit(solution)/shard_map/psum | solution.py:93
  307.8 1.6 multiply_convert_fusion.1
  309.4 0.0 all-to-all-done
  309.4 0.2 copy.15
  309.6 0.1 copy.16
  309.8 1.0 fusion.88
  (6 shorter events, 0.2 us)
Async XLA Ops:
  7.2 106.2 %copy-start.2 = (bf16[1,4,256,256]{3,2,1,0:T(8,128)(2,1)S(1)}, bf16[1,4,256,256]{3,2,1,0:T(8,128)(2,1)}, u32[]{:S(2)}) copy-start(bf16[1,4,256,256]{3,2,1,0:T(8,128)(2,1)} %param.9) | copy-start | bytes 1572868
  7.2 300.7 %all-reduce.3.cloned.1.call-start = ((), (), s32[]{:S(2)}) async-start(), calls=%async_computation.1 | async-start | bytes 7077888 | tf_op jit(solution)/shard_map/psum | solution.py:93
  94.4 14.5 %collective-permute-start = (bf16[2,4,256,128]{3,2,1,0:T(8,128)(2,1)S(1)}, bf16[2,4,256,128]{3,2,1,0:T(8,128)(2,1)S(1)}, u32[]{:S(2)}, u32[]{:S(2)}) collective-permute-start(bf16[2,4,256,128]{3,2,1,0:T(8,128)(2,1)S(1)} %fusion.87), channel_id=1, source_target_pairs={{0,16},{1,17},{2,18},{3,19},{4,20},{5,21},{6,22},{7,23},{8,24},{9,... | collective-permute-start | bytes 1572872 | tf_op jit(solution)/shard_map/ppermute | solution.py:15
  109.0 4.6 %collective-permute-start.2 = (bf16[4,1,256,128]{3,2,1,0:T(8,128)(2,1)S(1)}, bf16[4,1,256,128]{3,2,1,0:T(8,128)(2,1)S(1)}, u32[]{:S(2)}, u32[]{:S(2)}) collective-permute-start(bf16[4,1,256,128]{3,2,1,0:T(8,128)(2,1)S(1)} %get-tuple-element.5), channel_id=1, source_target_pairs={{1,0},{2,1},{3,2},{4,3},{5,4},{6,5},{7,6},{8,7},{9,8},{10,9},{11,1... | collective-permute-start | bytes 786440 | tf_op jit(solution)/shard_map/ppermute | solution.py:28
  110.3 4.2 %collective-permute-start.1 = (bf16[4,1,256,128]{3,2,1,0:T(8,128)(2,1)S(1)}, bf16[4,1,256,128]{3,2,1,0:T(8,128)(2,1)S(1)}, u32[]{:S(2)}, u32[]{:S(2)}) collective-permute-start(bf16[4,1,256,128]{3,2,1,0:T(8,128)(2,1)S(1)} %get-tuple-element.4), channel_id=1, source_target_pairs={{0,1},{1,2},{2,3},{3,4},{4,5},{5,6},{6,7},{7,8},{8,9},{9,10},{10,1... | collective-permute-start | bytes 786440 | tf_op jit(solution)/shard_map/ppermute | solution.py:26
  116.0 2.1 copy-start.1
  118.1 27.2 %copy-start = (bf16[4,6,256,384]{3,2,1,0:T(8,128)(2,1)}, bf16[4,6,256,384]{3,2,1,0:T(8,128)(2,1)S(1)}, u32[]{:S(2)}) copy-start(bf16[4,6,256,384]{3,2,1,0:T(8,128)(2,1)S(1)} %pad_maximum_fusion) | copy-start | bytes 14155780
  155.4 154.0 %all-to-all-start = ((bf16[2,4,256,256]{3,1,0,2:T(4,128)(2,1)}), bf16[2,4,256,256]{3,1,0,2:T(4,128)(2,1)S(1)}, u32[]{:S(2)}, u32[]{:S(2)}) async-start(bf16[2,4,256,256]{3,1,0,2:T(4,128)(2,1)} %copy.14), calls=%async_computation | async-start | bytes 2097152 | tf_op jit(solution)/shard_map/all_to_all | solution.py:78
Sparse Core Ops, SparseCore 0:
  147.0 160.7 all-reduce.2
where the time goes:
time: 318 us
  waiting for transfers between devices  155 us (49%)
  blocking collectives  82.2 us (26%)
  matrix products  35.4 us (11%)
  starting transfers between devices  17.3 us (5%)
  between operations  14.2 us (4%)
  other arithmetic  9.63 us (3%)
  local copies, waits for them, and re-layouts  4.02 us (1%)
    psum x1, waiting for transfers between devices, local(): summed = lax.psum(jnp.concatenate(blocks, axis=1), ('tm', 'height'))  144 us
    psum x1, blocking collectives, local(): group_mean = lax.psum(local_sums, ('tm', 'height')) / entries  42 us
    psum x1, blocking collectives, local(): lax.psum(jnp.sum(centered * centered, axis=(0, 2)), ('tm', 'height'))  40.2 us
    dot_general x9, matrix products, local(): jnp.einsum('frwk,kc->frcw', patches[tap_t:tap_t + frames, tap_r:tap_r + r...  21.8 us
    dot_general x9, matrix products, local(): jnp.einsum('frwk,frwc->ck', patches[tap_t:tap_t + frames, tap_r:tap_r + r...  13.6 us
    ppermute x1, waiting for transfers between devices, shifted(): lax.ppermute(value, axis, [(source, source + steps) for source in range(f...  10.2 us
    all_to_all x1, starting transfers between devices, local(): lax.all_to_all(conv_out, 'height', split_axis=2, concat_axis=1, tiled=True)  8.75 us
  transfers between devices with their start and end apart: 5, of which 3 were waited for; matrix products, arithmetic and copies ran while one was open for 3% of the time, Pallas kernels for 0%

commit v1 on v0

v1 whole, which is shorter than its diff:
```python
import functools
import math

import jax
import jax.numpy as jnp
from jax import lax
from jax.experimental import pallas as pl
from jax.experimental.pallas import tpu as pltpu
from jax.sharding import PartitionSpec as P

GROUPS = 32
KT = 3
MESH = pl.DeviceIdType.MESH
VMEM = pl.BlockSpec(memory_space=pltpu.VMEM)
BF16 = jnp.bfloat16
F32 = jnp.float32


def group_total(row, per_group):
    lane = lax.broadcasted_iota(jnp.int32, row.shape, 1)
    count = row.shape[1]
    span = 1
    while span < per_group:
        low = (lane % (2 * span)) < span
        row = row + jnp.where(low, pltpu.roll(row, count - span, 1), pltpu.roll(row, span, 1))
        span *= 2
    return row


def gather_kernel(n_time, n_rows, act, full, scale, mine, stats, halo_send, halo_recv, stat_send, stat_recv):
    time, height = lax.axis_index("tm"), lax.axis_index("height")
    frames, rows, width, channels = act.shape
    n_dev = n_time * n_rows
    me = time * n_rows + height

    barrier = pltpu.get_barrier_semaphore()

    def greet(step, carry):
        other = (me + step) % n_dev
        pl.semaphore_signal(barrier, inc=1, device_id=(other // n_rows, other % n_rows), device_id_type=MESH)
        return carry

    lax.fori_loop(1, n_dev, greet, 0)
    pl.semaphore_wait(barrier, n_dev - 1)

    top, bottom = pl.ds(0, 1), pl.ds(rows - 1, 1)
    has_up, has_down = height > 0, height < n_rows - 1
    has_next, has_prev = time < n_time - 1, time > 0
    up, down = height - 1, height + 1
    own, old = pl.ds(frames, frames), pl.ds(0, frames)
    everything = pl.ds(0, rows)
    moves = [
        (1, 0, everything, old, pl.ds(1, rows), has_next, has_prev),
        (1, -1, top, old, pl.ds(rows + 1, 1), has_next & has_up, has_prev & has_down),
        (1, 1, bottom, old, pl.ds(0, 1), has_next & has_down, has_prev & has_up),
        (0, -1, top, own, pl.ds(rows + 1, 1), has_up, has_down),
        (0, 1, bottom, own, pl.ds(0, 1), has_down, has_up),
    ]

    def halo(index):
        frame_step, row_step, source, to_frames, to_rows, sends, receives = moves[index]
        copy = pltpu.make_async_remote_copy(
            src_ref=act.at[:, source],
            dst_ref=full.at[to_frames, to_rows],
            send_sem=halo_send.at[index],
            recv_sem=halo_recv.at[index],
            device_id=(time + frame_step, height + row_step),
            device_id_type=MESH,
        )
        return copy, sends, receives

    for index in range(len(moves)):
        copy, sends, _ = halo(index)
        pl.when(sends)(copy.start)

    local = frames * rows * width
    chan_sum = jnp.zeros((1, channels), F32)
    for f in range(frames):
        for r in range(rows):
            chan_sum = chan_sum + jnp.sum(act[f, r].astype(F32), axis=0, keepdims=True)
    chan_mean = chan_sum * (1.0 / local)
    chan_dev = jnp.zeros((1, channels), F32)
    for f in range(frames):
        for r in range(rows):
            away = act[f, r].astype(F32) - chan_mean
            chan_dev = chan_dev + jnp.sum(away * away, axis=0, keepdims=True)
    packed = jnp.concatenate([chan_mean, chan_dev, jnp.zeros((6, channels), F32)], axis=0)
    mine[...] = packed
    stats[me] = packed

    def stat(step, slot, other):
        return pltpu.make_async_remote_copy(
            src_ref=mine,
            dst_ref=stats.at[slot],
            send_sem=stat_send.at[step],
            recv_sem=stat_recv.at[step],
            device_id=(other // n_rows, other % n_rows),
            device_id_type=MESH,
        )

    def send(step, carry):
        stat(step, me, (me + step) % n_dev).start()
        return carry

    lax.fori_loop(1, n_dev, send, 0)

    full[pl.ds(frames, frames), pl.ds(1, rows)] = act[...]
    zero_rows = jnp.zeros((2 * frames, 1, width, channels), BF16)

    @pl.when(jnp.logical_not(has_up))
    def _():
        full[:, pl.ds(0, 1)] = zero_rows

    @pl.when(jnp.logical_not(has_down))
    def _():
        full[:, pl.ds(rows + 1, 1)] = zero_rows

    def receive(step, carry):
        from_dev = (me + n_dev - step) % n_dev
        stat(step, from_dev, from_dev).wait_recv()
        return carry

    lax.fori_loop(1, n_dev, receive, 0)
    per_group = channels // GROUPS
    means, devs = stats[:, 0], stats[:, 1]
    mean = group_total(jnp.sum(means, axis=0, keepdims=True), per_group) * (1.0 / (n_dev * per_group))
    away = means - mean
    spread = jnp.sum(devs + local * (away * away), axis=0, keepdims=True)
    var = group_total(spread, per_group) * (1.0 / (local * n_dev * per_group))
    scale[...] = jnp.concatenate([mean, lax.rsqrt(var + 1e-06), jnp.zeros((6, channels), F32)], axis=0)

    for index in range(len(moves)):
        copy, sends, receives = halo(index)
        pl.when(receives)(copy.wait_recv)
        pl.when(sends)(copy.wait_send)

    @pl.when(jnp.logical_not(has_prev))
    def _():
        first = full[frames]
        for f in range(frames):
            full[f] = first

    def sent(step, carry):
        stat(step, me, (me + step) % n_dev).wait_send()
        return carry

    lax.fori_loop(1, n_dev, sent, 0)


def compute_kernel(dims, full, scale, gain, bias, weight, cot, pooled, grad, taps, cot_t):
    n_time, n_rows, outer, inner = dims
    height = lax.axis_index("height")
    n_pad, width, channels = full.shape[1:]
    rows = n_pad - 2
    n_out = weight.shape[1]
    own_rows = n_out // n_rows
    mean, factor, bias_row = scale[0:1], scale[1:2] * gain[...], bias[...]
    column = lax.broadcasted_iota(jnp.int32, (width, channels), 0)

    def prepare(r, carry):
        inside = jnp.logical_and(r + height > 0, r + height * rows < n_rows * rows + 1)
        keep = inside.astype(F32)

        def normed(f):
            v = (full[f, r].astype(F32) - mean) * factor + bias_row
            v = v / (1.0 + jnp.exp(-v))
            return v.astype(BF16).astype(F32) * keep

        frames = [normed(f) for f in range(4)]
        for t in range(KT):
            pair = frames[t] + frames[t + 1]
            left = jnp.where(column == 0, 0.0, pltpu.roll(pair, 1, 0))
            right = jnp.where(column == width - 1, 0.0, pltpu.roll(pair, width - 1, 0))
            base = pl.ds(pl.multiple_of(r * width, width), width)
            taps[t, base, 0:channels] = left.astype(BF16)
            taps[t, base, channels : 2 * channels] = pair.astype(BF16)
            taps[t, base, 2 * channels :] = right.astype(BF16)
        return carry

    lax.fori_loop(0, n_pad, prepare, 0)

    def conv(y, carry):
        patch = jnp.concatenate(
            [taps[t, pl.ds(pl.multiple_of((y + r) * width, width), width)] for t in range(KT) for r in range(KT)], axis=1
        )
        out = jnp.dot(patch, weight[...], preferred_element_type=F32) * 0.5
        pooled[:, y] = out.T.astype(BF16).reshape(n_rows, own_rows, width)
        cot_t[:, pl.ds(pl.multiple_of(y * width, width), width)] = cot[y].astype(F32).T.astype(BF16)
        return carry

    lax.fori_loop(0, rows, conv, 0)
    span = grad.shape[-1]
    upstream = cot_t[...]
    pixels = rows * width
    band = KT * KT * channels
    for t in range(KT):
        rhs = jnp.concatenate([taps[t, pl.ds(r * width, pixels)] for r in range(KT)], axis=1)
        total = jnp.dot(upstream, rhs, preferred_element_type=F32).astype(BF16)
        for piece in range(n_time):
            first, last = max(t * band, piece * span), min((t + 1) * band, (piece + 1) * span)
            if first < last:
                part = total[:, first - t * band : last - t * band]
                for block in range(n_rows):
                    q, core = block // 2, block % 2
                    grad[core, piece, q % inner, q // inner, :, first - piece * span : last - piece * span] = part[
                        block * own_rows : (block + 1) * own_rows
                    ]
    extra = n_time * span - KT * band
    if extra:
        for piece in range(n_time):
            first = max(KT * band, piece * span) - piece * span
            if first < span:
                grad[:, piece, :, :, :, first:] = jnp.zeros((2, inner, outer, own_rows, span - first), BF16)


def scatter_kernel(
    dims, factor, pooled, grad, out, wgrad, got1, sum1, got2, sum2, got3, part, sems_a, semr_a, sems, semr, final
):
    n_time, n_rows, outer, inner = dims
    time, height = lax.axis_index("tm"), lax.axis_index("height")
    core, q = height % 2, height // 2
    b, a = q % inner, q // inner
    rows = pooled.shape[1]

    def index_of(a_, b_, c_):
        return (a_ * inner + b_) * 2 + c_

    def remote(src, dst, index, to):
        return pltpu.make_async_remote_copy(
            src_ref=src, dst_ref=dst, send_sem=sems.at[index], recv_sem=semr.at[index], device_id=to, device_id_type=MESH
        )

    barrier = pltpu.get_barrier_semaphore()
    for step in range(1, n_rows):
        pl.semaphore_signal(barrier, inc=1, device_id=(time, (height + step) % n_rows), device_id_type=MESH)
    for t in range(1, n_time):
        for b_ in range(inner):
            pl.semaphore_signal(
                barrier, inc=1, device_id=((time + t) % n_time, index_of(a, b_, core)), device_id_type=MESH
            )
    pl.semaphore_wait(barrier, n_rows - 1 + (n_time - 1) * inner)

    pair = remote(grad.at[1 - core], got1, 0, (time, index_of(a, b, 1 - core)))
    pair.start()

    def block(step, slot, other):
        return pltpu.make_async_remote_copy(
            src_ref=pooled.at[other],
            dst_ref=out.at[pl.ds(slot * rows, rows)],
            send_sem=sems_a.at[step],
            recv_sem=semr_a.at[step],
            device_id=(time, other),
            device_id_type=MESH,
        )

    for step in range(1, n_rows):
        block(step, height, (height + step) % n_rows).start()
    out[pl.ds(height * rows, rows)] = pooled[height]

    pair.wait()
    for t in range(n_time):
        for b_ in range(inner):
            for a_ in range(outer):
                sum1[t, b_, a_] = (grad[core, t, b_, a_].astype(F32) + got1[t, b_, a_].astype(F32)).astype(BF16)

    def second(dt, db, backward):
        sign = -1 if backward else 1
        t_, b_ = (time + n_time + sign * dt) % n_time, (b + inner + sign * db) % inner
        slot = dt * inner + db - 1
        return remote(sum1.at[t_, b_], got2.at[slot], 1 + slot, (t_, index_of(a, b_, core)))

    group = [(dt, db) for dt in range(n_time) for db in range(inner) if dt or db]
    seconds = [second(dt, db, False) for dt, db in group]
    for copy in seconds:
        copy.start()
    for copy in seconds:
        copy.wait_recv()
    for a_ in range(outer):
        total = sum1[time, b, a_].astype(F32)
        for slot in range(len(group)):
            total = total + got2[slot, a_].astype(F32)
        sum2[a_] = total.astype(BF16)

    base = 1 + len(group)
    thirds = []
    for step in range(1, outer):
        a_ = (a + step) % outer
        thirds.append(remote(sum2.at[a_], got3.at[step - 1], base + step - 1, (time, index_of(a_, b, core))))
    for copy in thirds:
        copy.start()
    for copy in thirds:
        copy.wait_recv()
    total = sum2[a].astype(F32)
    for step in range(1, outer):
        total = total + got3[step - 1].astype(F32)
    part[...] = (total * factor).astype(BF16)
    final[time] = part[...]

    base = base + outer - 1
    lasts = []
    for t in range(1, n_time):
        lasts.append((t, remote(part, final.at[time], base + t - 1, ((time + t) % n_time, height))))
    for _, copy in lasts:
        copy.start()
    for t, _ in lasts:
        sender = (time + n_time - t) % n_time
        remote(part, final.at[sender], base + t - 1, (sender, height)).wait_recv()
    whole = jnp.concatenate([final[t] for t in range(n_time)], axis=1)
    wgrad[...] = whole[:, : wgrad.shape[1]]

    for copy in seconds + thirds + [c for _, c in lasts]:
        copy.wait_send()
    for step in range(1, n_rows):
        sender = (height + n_rows - step) % n_rows
        block(step, sender, sender).wait_recv()
        block(step, height, (height + step) % n_rows).wait_send()


def local(activations, norm_gain, norm_bias, conv_weight, cotangent):
    frames, rows, width, channels = activations.shape
    depth, n_out = conv_weight.shape
    n_time, n_rows = lax.axis_size("tm"), lax.axis_size("height")
    n_dev = n_time * n_rows
    inner = 2
    outer = n_rows // (2 * inner)
    own_rows = n_out // n_rows
    dims = (n_time, n_rows, outer, inner)
    span = -(-depth // (128 * n_time)) * 128
    dma = pltpu.SemaphoreType.DMA

    full, scale = pl.pallas_call(
        functools.partial(gather_kernel, n_time, n_rows),
        out_shape=(
            jax.ShapeDtypeStruct((2 * frames, rows + 2, width, channels), BF16),
            jax.ShapeDtypeStruct((8, channels), F32),
        ),
        in_specs=[VMEM],
        out_specs=(VMEM, VMEM),
        scratch_shapes=[
            pltpu.VMEM((8, channels), F32),
            pltpu.VMEM((n_dev, 8, channels), F32),
            dma((5,)),
            dma((5,)),
            dma((n_dev,)),
            dma((n_dev,)),
        ],
        compiler_params=pltpu.CompilerParams(collective_id=0, has_side_effects=True, vmem_limit_bytes=40 << 20),
        name="gather",
    )(activations)

    pooled, grad = pl.pallas_call(
        functools.partial(compute_kernel, dims),
        out_shape=(
            jax.ShapeDtypeStruct((n_rows, rows, own_rows, width), BF16),
            jax.ShapeDtypeStruct((2, n_time, inner, outer, own_rows, span), BF16),
        ),
        in_specs=[VMEM] * 6,
        out_specs=(VMEM, VMEM),
        scratch_shapes=[
            pltpu.VMEM((KT, (rows + 2) * width, KT * channels), BF16),
            pltpu.VMEM((n_out, rows * width), BF16),
        ],
        compiler_params=pltpu.CompilerParams(vmem_limit_bytes=48 << 20),
        name="compute",
    )(
        full,
        scale,
        norm_gain.reshape(1, channels),
        norm_bias.reshape(1, channels),
        conv_weight,
        cotangent.reshape(rows, width, n_out),
    )

    factor = 0.5 / math.sqrt(frames * n_time * rows * n_rows * width)
    n_sems = n_time * inner + outer + n_time
    out, weight_grad = pl.pallas_call(
        functools.partial(scatter_kernel, dims, factor),
        out_shape=(
            jax.ShapeDtypeStruct((rows * n_rows, own_rows, width), BF16),
            jax.ShapeDtypeStruct((own_rows, depth), BF16),
        ),
        in_specs=[VMEM, VMEM],
        out_specs=(VMEM, VMEM),
        scratch_shapes=[
            pltpu.VMEM((n_time, inner, outer, own_rows, span), BF16),
            pltpu.VMEM((n_time, inner, outer, own_rows, span), BF16),
            pltpu.VMEM((n_time * inner - 1, outer, own_rows, span), BF16),
            pltpu.VMEM((outer, own_rows, span), BF16),
            pltpu.VMEM((outer - 1, own_rows, span), BF16),
            pltpu.VMEM((own_rows, span), BF16),
            dma((n_rows,)),
            dma((n_rows,)),
            dma((n_sems,)),
            dma((n_sems,)),
            pltpu.VMEM((n_time, own_rows, span), BF16),
        ],
        compiler_params=pltpu.CompilerParams(collective_id=1, has_side_effects=True, vmem_limit_bytes=40 << 20),
        name="scatter",
    )(pooled, grad)
    return (out.reshape((1,) + out.shape), weight_grad)


def solution(mesh):
    in_specs = (P("tm", "height", None, None), P(), P(), P(), P("tm", "height", None, None))
    out_specs = (P("tm", None, "height", None), P("height", None))
    return jax.shard_map(local, mesh=mesh, in_specs=in_specs, out_specs=out_specs, check_vma=False)
```

time: 318 us -> 73.7 us (0.23)
  waiting for transfers between devices: 155 us -> 0 us
  blocking collectives: 82.2 us -> 0 us
  Pallas kernels: 0 us -> 65 us
  matrix products: 35.4 us -> 0 us
  starting transfers between devices: 17.3 us -> 0 us
  between operations: 14.2 us -> 0.67 us
  other arithmetic: 9.63 us -> 0 us
  local copies, waits for them, and re-layouts: 4.02 us -> 7.8 us
    psum x1 -> x0, waiting for transfers between devices: 144 us -> none  [local(): summed = lax.psum(jnp.concatenate(blocks, axis=1), ('tm', 'height'))]
    psum x2 -> x0, blocking collectives: 82.2 us -> none  [the longest x1 42 us: local(): group_mean = lax.psum(local_sums, ('tm', 'height')) / entries]
    pallas_call x0 -> x3, Pallas kernels: none -> 65 us  [the longest x1 31.4 us: local(): pl.pallas_call(functools.partial(scatter_kernel, dims, factor), out_shape...]
    dot_general x18 -> x0, matrix products: 35.4 us -> none  [the longest x9 21.8 us: local(): jnp.einsum('frwk,kc->frcw', patches[tap_t:tap_t + frames, tap_r:tap_r + r...]
    ppermute x3 -> x0, waiting for transfers between devices: 11.1 us -> none  [the longest x1 10.2 us: shifted(): lax.ppermute(value, axis, [(source, source + steps) for source in range(f...]
    all_to_all x1 -> x0, starting transfers between devices: 8.75 us -> none  [local(): lax.all_to_all(conv_out, 'height', split_axis=2, concat_axis=1, tiled=True)]
    ppermute x3 -> x0, starting transfers between devices: 8.54 us -> none  [the longest x1 4.21 us: shifted(): lax.ppermute(value, axis, [(source, source + steps) for source in range(f...]
    unnamed x6 -> x14, local copies, waits for them, and re-layouts: 0.01 us -> 7.8 us
  transfers between devices with their start and end apart: 5 -> 0, of which waited for: 3 -> 0; matrix products, arithmetic and copies ran while one was open for 3% -> 0% of each run, Pallas kernels for 0% -> 0%
where the time goes in v1:
time: 73.7 us; the launch traced here: 73.4 us
  Pallas kernels  65 us (88%)
  local copies, waits for them, and re-layouts  7.8 us (11%)
    pallas_call x1, Pallas kernels, local(): pl.pallas_call(functools.partial(scatter_kernel, dims, factor), out_shape...  31.4 us
    pallas_call x1, Pallas kernels, local(): pl.pallas_call(functools.partial(gather_kernel, n_time, n_rows), out_shap...  25.2 us
    pallas_call x1, Pallas kernels, local(): pl.pallas_call(functools.partial(compute_kernel, dims), out_shape=(jax.Sh...  8.37 us
    unnamed x14, local copies, waits for them, and re-layouts  7.8 us

profile of v1, /device:TPU:0, one launch (start us, length us, event | category | flops | bytes accessed | tf_op | source)
XLA Modules:
  0.0 73.4 jit_solution(2037034136457178174)
XLA Ops:
  0.6 0.0 copy-start.3
  0.6 1.0 %copy-done.3 = bf16[2,4,256,128]{3,2,1,0:T(8,128)(2,1)S(1)} copy-done((bf16[2,4,256,128]{3,2,1,0:T(8,128)(2,1)S(1)}, bf16[2,4,256,128]{3,2,1,0:T(8,128)(2,1)}, u32[]{:S(2)}) %copy-start.3) | copy-done | bytes 524312
  1.7 25.2 %gather.1 = (bf16[4,6,256,128]{3,2,1,0:T(8,128)(2,1)S(1)}, f32[8,128]{1,0:T(8,128)S(1)}) custom-call(bf16[2,4,256,128]{3,2,1,0:T(8,128)(2,1)S(1)} %copy-done.3), custom_call_target="tpu_custom_call" | custom-call | tf_op jit(solution)/shard_map/gather/pallas_call | solution.py:331
  26.9 0.0 copy-start.1
  26.9 1.5 %copy-done.1 = bf16[3456,256]{1,0:T(8,128)(2,1)S(1)} copy-done((bf16[3456,256]{1,0:T(8,128)(2,1)S(1)}, bf16[3456,256]{1,0:T(8,128)(2,1)}, u32[]{:S(2)}) %copy-start.1) | copy-done | bytes 1769496
  28.4 0.0 copy-start.2
  28.4 1.0 %copy-done.2 = bf16[1,4,256,256]{3,2,1,0:T(8,128)(2,1)S(1)} copy-done((bf16[1,4,256,256]{3,2,1,0:T(8,128)(2,1)S(1)}, bf16[1,4,256,256]{3,2,1,0:T(8,128)(2,1)}, u32[]{:S(2)}) %copy-start.2) | copy-done | bytes 524312
  29.4 0.0 copy-start.4
  29.4 0.7 copy-done.4
  30.1 0.0 copy-start.5
  30.1 0.7 copy-done.5
  30.7 8.4 %compute.1 = (bf16[16,4,16,256]{3,2,1,0:T(8,128)(2,1)S(1)}, bf16[2,2,2,4,16,1792]{5,4,3,2,1,0:T(8,128)(2,1)}) custom-call(bf16[4,6,256,128]{3,2,1,0:T(8,128)(2,1)S(1)} %get-tuple-element.8.full, f32[8,128]{1,0:T(8,128)S(1)} %get-tuple-element.9.scale, f32[1,128]{1,0:T(1,128)S(1)} %bitcast.6, f32[1,128]{1,0:T(1,128)S(1)} %bitcast.7, ...), custom_call_target="tpu_custom_call" | custom-call | tf_op jit(solution)/shard_map/compute/pallas_call | solution.py:351
  39.1 0.0 copy-start
  39.1 1.5 %copy-done = bf16[2,2,2,4,16,1792]{5,4,3,2,1,0:T(8,128)(2,1)S(1)} copy-done((bf16[2,2,2,4,16,1792]{5,4,3,2,1,0:T(8,128)(2,1)S(1)}, bf16[2,2,2,4,16,1792]{5,4,3,2,1,0:T(8,128)(2,1)}, u32[]{:S(2)}) %copy-start) | copy-done | bytes 1835032
  40.6 31.4 %scatter.1 = (bf16[64,16,256]{2,1,0:T(8,128)(2,1)S(1)}, bf16[16,3456]{1,0:T(8,128)(2,1)S(1)}) custom-call(bf16[16,4,16,256]{3,2,1,0:T(8,128)(2,1)S(1)} %get-tuple-element.10.pooled, bf16[2,2,2,4,16,1792]{5,4,3,2,1,0:T(8,128)(2,1)S(1)} %copy-done), custom_call_target="tpu_custom_call" | custom-call | tf_op jit(solution)/shard_map/scatter/pallas_call | solution.py:376
  72.0 0.8 %copy.9 = bf16[1,64,16,256]{3,2,1,0:T(8,128)(2,1)} copy(bf16[1,64,16,256]{3,2,1,0:T(8,128)(2,1)S(1)} %bitcast.5) | data formatting | bytes 1048576
  72.8 0.6 copy.10
Async XLA Ops:
  0.6 1.0 %copy-start.3 = (bf16[2,4,256,128]{3,2,1,0:T(8,128)(2,1)S(1)}, bf16[2,4,256,128]{3,2,1,0:T(8,128)(2,1)}, u32[]{:S(2)}) copy-start(bf16[2,4,256,128]{3,2,1,0:T(8,128)(2,1)} %act.1) | copy-start | bytes 1572868
  26.9 1.5 %copy-start.1 = (bf16[3456,256]{1,0:T(8,128)(2,1)S(1)}, bf16[3456,256]{1,0:T(8,128)(2,1)}, u32[]{:S(2)}) copy-start(bf16[3456,256]{1,0:T(8,128)(2,1)} %weight.1) | copy-start | bytes 5308420
  28.4 1.0 %copy-start.2 = (bf16[1,4,256,256]{3,2,1,0:T(8,128)(2,1)S(1)}, bf16[1,4,256,256]{3,2,1,0:T(8,128)(2,1)}, u32[]{:S(2)}) copy-start(bf16[1,4,256,256]{3,2,1,0:T(8,128)(2,1)} %param.9) | copy-start | bytes 1572868
  29.4 0.7 copy-start.4
  30.1 0.7 copy-start.5
  39.1 1.5 %copy-start = (bf16[2,2,2,4,16,1792]{5,4,3,2,1,0:T(8,128)(2,1)S(1)}, bf16[2,2,2,4,16,1792]{5,4,3,2,1,0:T(8,128)(2,1)}, u32[]{:S(2)}) copy-start(bf16[2,2,2,4,16,1792]{5,4,3,2,1,0:T(8,128)(2,1)} %get-tuple-element.11.grad) | copy-start | bytes 5505028

commit v2 on v0

v2 whole, which is shorter than its diff:
```python
import functools
import math

import jax
import jax.numpy as jnp
from jax import lax
from jax.experimental import pallas as pl
from jax.experimental.pallas import tpu as pltpu
from jax.sharding import PartitionSpec as P

GROUPS = 32
KT = 3
MESH = pl.DeviceIdType.MESH
ANY = pl.BlockSpec(memory_space=pl.ANY)
VMEM = pl.BlockSpec(memory_space=pltpu.VMEM)
BF16 = jnp.bfloat16
F32 = jnp.float32


def group_total(row, per_group):
    lane = lax.broadcasted_iota(jnp.int32, row.shape, 1)
    count = row.shape[1]
    span = 1
    while span < per_group:
        low = (lane % (2 * span)) < span
        row = row + jnp.where(low, pltpu.roll(row, count - span, 1), pltpu.roll(row, span, 1))
        span *= 2
    return row


def index_of(inner, a, b, core):
    return (a * inner + b) * 2 + core


class Stream:
    def __init__(self, dims, place, refs, sems):
        self.dims, self.place = dims, place
        self.grad, self.got1, self.sum1, self.got2, self.sum2, self.got3, self.part, self.final = refs
        self.send_sem, self.recv_sem = sems

    def remote(self, src, dst, index, to):
        return pltpu.make_async_remote_copy(
            src_ref=src,
            dst_ref=dst,
            send_sem=self.send_sem.at[index],
            recv_sem=self.recv_sem.at[index],
            device_id=to,
            device_id_type=MESH,
        )

    def start_pair(self):
        n_time, n_rows, outer, inner = self.dims
        time, height, a, b, core = self.place
        self.pair = self.remote(self.grad.at[1 - core], self.got1, 0, (time, index_of(inner, a, b, 1 - core)))
        self.pair.start()

    def start_second(self):
        n_time, n_rows, outer, inner = self.dims
        time, height, a, b, core = self.place
        self.pair.wait()
        for t in range(n_time):
            for b_ in range(inner):
                for a_ in range(outer):
                    self.sum1[t, b_, a_] = (
                        self.grad[core, t, b_, a_].astype(F32) + self.got1[t, b_, a_].astype(F32)
                    ).astype(BF16)
        self.seconds = []
        for dt in range(n_time):
            for db in range(inner):
                if dt or db:
                    slot = dt * inner + db - 1
                    t_, b_ = (time + dt) % n_time, (b + db) % inner
                    self.seconds.append(
                        self.remote(
                            self.sum1.at[t_, b_], self.got2.at[slot], 1 + slot, (t_, index_of(inner, a, b_, core))
                        )
                    )
        for copy in self.seconds:
            copy.start()

    def start_third(self):
        n_time, n_rows, outer, inner = self.dims
        time, height, a, b, core = self.place
        for copy in self.seconds:
            copy.wait_recv()
        for a_ in range(outer):
            total = self.grad[core, time, b, a_].astype(F32) + self.got1[time, b, a_].astype(F32)
            for slot in range(n_time * inner - 1):
                total = total + self.got2[slot, a_].astype(F32)
            self.sum2[a_] = total.astype(BF16)
        self.thirds = []
        for step in range(1, outer):
            a_ = (a + step) % outer
            self.thirds.append(
                self.remote(
                    self.sum2.at[a_],
                    self.got3.at[step - 1],
                    n_time * inner + step - 1,
                    (time, index_of(inner, a_, b, core)),
                )
            )
        for copy in self.thirds:
            copy.start()

    def start_last(self, factor):
        n_time, n_rows, outer, inner = self.dims
        time, height, a, b, core = self.place
        for copy in self.thirds:
            copy.wait_recv()
        total = self.sum2[a].astype(F32)
        for step in range(1, outer):
            total = total + self.got3[step - 1].astype(F32)
        self.part[...] = (total * factor).astype(BF16)
        self.final[time] = self.part[...]
        self.base = n_time * inner + outer - 1
        self.lasts = []
        for t in range(1, n_time):
            self.lasts.append(
                self.remote(self.part, self.final.at[time], self.base + t - 1, ((time + t) % n_time, height))
            )
        for copy in self.lasts:
            copy.start()

    def finish(self):
        n_time = self.dims[0]
        time, height = self.place[:2]
        for t in range(1, n_time):
            sender = (time + n_time - t) % n_time
            self.remote(self.part, self.final.at[sender], self.base + t - 1, (sender, height)).wait_recv()
        whole = jnp.concatenate([self.final[t] for t in range(n_time)], axis=1)
        for copy in self.seconds + self.thirds + self.lasts:
            copy.wait_send()
        return whole


def block_kernel(dims, factor, act, gain_in, bias_in, weight_in, cot_in, out, wgrad, *scratch):
    n_time, n_rows, outer, inner = dims
    full, first, taps, acc, gain, bias, weight, cot, cot_t, mine, stats, pooled = scratch[:12]
    local_sem, halo_send, halo_recv, stat_send, stat_recv, block_send, block_recv = scratch[12:19]
    late_refs, late_sems = scratch[19:27], scratch[27:29]
    early_refs, early_sems = scratch[29:37], scratch[37:39]
    time, height = lax.axis_index("tm"), lax.axis_index("height")
    frames, rows, width, channels = act.shape
    n_out = weight.shape[1]
    own_rows = n_out // n_rows
    pixels = rows * width
    n_dev = n_time * n_rows
    me = time * n_rows + height
    core, q = height % 2, height // 2
    place = (time, height, q // inner, q % inner, core)
    late = Stream(dims, place, late_refs, late_sems)
    early = Stream(dims, place, early_refs, early_sems)

    own_frames, old_frames = pl.ds(frames, frames), pl.ds(0, frames)
    loads = [
        pltpu.make_async_copy(act, full.at[own_frames, pl.ds(1, rows)], local_sem.at[0]),
        pltpu.make_async_copy(gain_in, gain, local_sem.at[1]),
        pltpu.make_async_copy(bias_in, bias, local_sem.at[2]),
        pltpu.make_async_copy(cot_in, cot, local_sem.at[3]),
        pltpu.make_async_copy(weight_in, weight, local_sem.at[4]),
    ]
    for load in loads:
        load.start()

    barrier = pltpu.get_barrier_semaphore()

    def greet(step, carry):
        other = (me + step) % n_dev
        pl.semaphore_signal(barrier, inc=1, device_id=(other // n_rows, other % n_rows), device_id_type=MESH)
        return carry

    lax.fori_loop(1, n_dev, greet, 0)

    loads[0].wait()
    local = frames * pixels
    chan_sum = jnp.zeros((1, channels), F32)
    for f in range(frames):
        for r in range(rows):
            chan_sum = chan_sum + jnp.sum(full[frames + f, 1 + r].astype(F32), axis=0, keepdims=True)
    chan_mean = chan_sum * (1.0 / local)
    chan_dev = jnp.zeros((1, channels), F32)
    for f in range(frames):
        for r in range(rows):
            away = full[frames + f, 1 + r].astype(F32) - chan_mean
            chan_dev = chan_dev + jnp.sum(away * away, axis=0, keepdims=True)
    packed = jnp.concatenate([chan_mean, chan_dev, jnp.zeros((6, channels), F32)], axis=0)
    mine[...] = packed
    stats[me] = packed
    pl.semaphore_wait(barrier, n_dev - 1)

    def stat(step, slot, to_time, to_height):
        return pltpu.make_async_remote_copy(
            src_ref=mine,
            dst_ref=stats.at[slot],
            send_sem=stat_send.at[step],
            recv_sem=stat_recv.at[step],
            device_id=(to_time, to_height),
            device_id_type=MESH,
        )

    def stat_out(step):
        return stat(step, me, (time + step // n_rows) % n_time, (height + step % n_rows) % n_rows)

    def send(step, carry):
        stat_out(step).start()
        return carry

    has_up, has_down = height > 0, height < n_rows - 1
    has_next, has_prev = time < n_time - 1, time > 0
    moves = [
        (own_frames, 1, 1, old_frames, 1, 1, 0, has_next, has_prev),
        (own_frames, rows, 1, old_frames, rows, 1, 0, has_next, has_prev),
        (own_frames, 2, rows - 2, old_frames, 2, 1, 0, has_next, has_prev),
        (own_frames, 1, 1, own_frames, rows + 1, 0, -1, has_up, has_down),
        (own_frames, rows, 1, own_frames, 0, 0, 1, has_down, has_up),
        (old_frames, 1, 1, old_frames, rows + 1, 0, -1, has_prev & has_up, has_prev & has_down),
        (old_frames, rows, 1, old_frames, 0, 0, 1, has_prev & has_down, has_prev & has_up),
    ]

    def halo(index):
        from_frames, from_row, count, to_frames, to_row, frame_step, row_step = moves[index][:7]
        return pltpu.make_async_remote_copy(
            src_ref=full.at[from_frames, pl.ds(from_row, count)],
            dst_ref=full.at[to_frames, pl.ds(to_row, count)],
            send_sem=halo_send.at[index],
            recv_sem=halo_recv.at[index],
            device_id=(time + frame_step, height + row_step),
            device_id_type=MESH,
        )

    def start(index):
        pl.when(moves[index][7])(lambda: halo(index).start())

    def arrived(index):
        pl.when(moves[index][8])(lambda: halo(index).wait_recv())

    lax.fori_loop(n_rows, n_dev, send, 0)
    for index in range(5):
        start(index)
    lax.fori_loop(1, n_rows, send, 0)

    zero_rows = jnp.zeros((2 * frames, 1, width, channels), BF16)

    @pl.when(jnp.logical_not(has_up))
    def _():
        full[:, pl.ds(0, 1)] = zero_rows

    @pl.when(jnp.logical_not(has_down))
    def _():
        full[:, pl.ds(rows + 1, 1)] = zero_rows

    loads[3].wait()
    for y in range(rows):
        cot_t[:, y * width : (y + 1) * width] = cot[y].astype(F32).T.astype(BF16)
    for index in (1, 2, 4):
        loads[index].wait()

    def receive(step, carry):
        from_time = (time + n_time - step // n_rows) % n_time
        from_height = (height + n_rows - step % n_rows) % n_rows
        stat(step, from_time * n_rows + from_height, from_time, from_height).wait_recv()
        return carry

    lax.fori_loop(1, n_dev, receive, 0)
    per_group = channels // GROUPS
    means, devs = stats[:, 0], stats[:, 1]
    mean = group_total(jnp.sum(means, axis=0, keepdims=True), per_group) * (1.0 / (n_dev * per_group))
    away = means - mean
    spread = jnp.sum(devs + local * (away * away), axis=0, keepdims=True)
    var = group_total(spread, per_group) * (1.0 / (local * n_dev * per_group))
    scale = lax.rsqrt(var + 1e-06) * gain[...]
    shift = bias[...]
    column = lax.broadcasted_iota(jnp.int32, (width, channels), 0)

    def normed(f, r):
        inside = jnp.logical_and(r + height > 0, r + height * rows < n_rows * rows + 1)
        v = (full[f, r].astype(F32) - mean) * scale + shift
        v = v / (1.0 + jnp.exp(-v))
        return v.astype(BF16).astype(F32) * inside.astype(F32)

    def put(t, r, pair):
        left = jnp.where(column == 0, 0.0, pltpu.roll(pair, 1, 0))
        right = jnp.where(column == width - 1, 0.0, pltpu.roll(pair, width - 1, 0))
        base = pl.ds(pl.multiple_of(r * width, width), width)
        taps[t, base, 0:channels] = left.astype(BF16)
        taps[t, base, channels : 2 * channels] = pair.astype(BF16)
        taps[t, base, 2 * channels :] = right.astype(BF16)

    def prepare_own(r, carry):
        one, two = normed(frames, r), normed(frames + 1, r)
        first[r] = one.astype(BF16)
        put(2, r, one + two)
        return carry

    arrived(3)
    arrived(4)
    lax.fori_loop(0, rows + 2, prepare_own, 0)

    def product(stream, t, offset, length):
        band = KT * KT * channels
        span = stream.grad.shape[-1]
        rhs = jnp.concatenate([taps[t, pl.ds(r * width, pixels)] for r in range(KT)], axis=1)
        total = jnp.dot(cot_t[...], rhs, preferred_element_type=F32).astype(BF16)
        for piece in range(n_time):
            begin, end = max(offset, piece * span), min(offset + band, (piece + 1) * span)
            if begin < end:
                part = total[:, begin - offset : end - offset]
                for block in range(n_rows):
                    q_, core_ = block // 2, block % 2
                    stream.grad[
                        core_, piece, q_ % inner, q_ // inner, :, begin - piece * span : end - piece * span
                    ] = part[block * own_rows : (block + 1) * own_rows]
            unused = max(length, piece * span) - piece * span
            if offset + band == length and unused < span:
                stream.grad[:, piece, :, :, :, unused:] = jnp.zeros((2, inner, outer, own_rows, span - unused), BF16)

    band = KT * KT * channels
    product(early, 2, 0, band)
    early.start_pair()

    arrived(0)
    start(5)
    arrived(1)
    start(6)

    def patch(t, y):
        return [taps[t, pl.ds(pl.multiple_of((y + r) * width, width), width)] for r in range(KT)]

    def conv_own(y, carry):
        acc[y] = jnp.dot(jnp.concatenate(patch(2, y), axis=1), weight[2 * band :], preferred_element_type=F32)
        return carry

    lax.fori_loop(0, rows, conv_own, 0)
    early.start_second()

    for index in (2, 5, 6):
        arrived(index)

    @pl.when(jnp.logical_not(has_prev))
    def _():
        for f in range(frames):
            full[f] = full[frames]

    def prepare_old(r, carry):
        one, two = normed(0, r), normed(1, r)
        put(0, r, one + two)
        put(1, r, two + first[r].astype(F32))
        return carry

    lax.fori_loop(0, rows + 2, prepare_old, 0)

    def conv_old(y, carry):
        lhs = jnp.concatenate(patch(0, y) + patch(1, y), axis=1)
        total = (acc[y] + jnp.dot(lhs, weight[0 : 2 * band], preferred_element_type=F32)) * 0.5
        pooled[:, y] = total.T.astype(BF16).reshape(n_rows, own_rows, width)
        return carry

    lax.fori_loop(0, rows, conv_old, 0)

    def block(step, slot, other):
        return pltpu.make_async_remote_copy(
            src_ref=pooled.at[other],
            dst_ref=out.at[pl.ds(slot * rows, rows)],
            send_sem=block_send.at[step],
            recv_sem=block_recv.at[step],
            device_id=(time, other),
            device_id_type=MESH,
        )

    for step in range(1, n_rows):
        block(step, height, (height + step) % n_rows).start()
    product(late, 0, 0, 2 * band)
    product(late, 1, band, 2 * band)
    late.start_pair()
    out[pl.ds(height * rows, rows)] = pooled[height]
    early.start_third()
    late.start_second()
    early.start_last(factor)
    late.start_third()
    wgrad[:, 2 * band :] = early.finish()[:, :band]
    late.start_last(factor)
    wgrad[:, : 2 * band] = late.finish()[:, : 2 * band]

    for step in range(1, n_rows):
        sender = (height + n_rows - step) % n_rows
        block(step, sender, sender).wait_recv()
        block(step, height, (height + step) % n_rows).wait_send()
    for index in range(len(moves)):
        pl.when(moves[index][7])(functools.partial(lambda i: halo(i).wait_send(), index))

    def sent(step, carry):
        stat_out(step).wait_send()
        return carry

    lax.fori_loop(1, n_dev, sent, 0)


def local(activations, norm_gain, norm_bias, conv_weight, cotangent):
    frames, rows, width, channels = activations.shape
    depth, n_out = conv_weight.shape
    n_time, n_rows = lax.axis_size("tm"), lax.axis_size("height")
    n_dev = n_time * n_rows
    inner = 2
    outer = n_rows // (2 * inner)
    own_rows = n_out // n_rows
    dims = (n_time, n_rows, outer, inner)
    dma = pltpu.SemaphoreType.DMA
    factor = 0.5 / math.sqrt(frames * n_time * rows * n_rows * width)

    def stream(length):
        span = -(-length // (128 * n_time)) * 128
        n_sems = n_time * inner + outer + n_time
        shapes = [
            (2, n_time, inner, outer, own_rows, span),
            (n_time, inner, outer, own_rows, span),
            (n_time, inner, outer, own_rows, span),
            (n_time * inner - 1, outer, own_rows, span),
            (outer, own_rows, span),
            (outer - 1, own_rows, span),
            (own_rows, span),
            (n_time, own_rows, span),
        ]
        return [pltpu.VMEM(shape, BF16) for shape in shapes] + [dma((n_sems,)), dma((n_sems,))]

    band = depth // KT
    out, weight_grad = pl.pallas_call(
        functools.partial(block_kernel, dims, factor),
        out_shape=(
            jax.ShapeDtypeStruct((rows * n_rows, own_rows, width), BF16),
            jax.ShapeDtypeStruct((own_rows, depth), BF16),
        ),
        in_specs=[ANY] * 5,
        out_specs=(VMEM, VMEM),
        scratch_shapes=[
            pltpu.VMEM((2 * frames, rows + 2, width, channels), BF16),
            pltpu.VMEM((rows + 2, width, channels), BF16),
            pltpu.VMEM((KT, (rows + 2) * width, KT * channels), BF16),
            pltpu.VMEM((rows, width, n_out), F32),
            pltpu.VMEM((1, channels), F32),
            pltpu.VMEM((1, channels), F32),
            pltpu.VMEM((depth, n_out), BF16),
            pltpu.VMEM((rows, width, n_out), BF16),
            pltpu.VMEM((n_out, rows * width), BF16),
            pltpu.VMEM((8, channels), F32),
            pltpu.VMEM((n_dev, 8, channels), F32),
            pltpu.VMEM((n_rows, rows, own_rows, width), BF16),
            dma((5,)),
            dma((7,)),
            dma((7,)),
            dma((n_dev,)),
            dma((n_dev,)),
            dma((n_rows,)),
            dma((n_rows,)),
            *stream(2 * band),
            *stream(band),
        ],
        compiler_params=pltpu.CompilerParams(collective_id=0, has_side_effects=True, vmem_limit_bytes=56 << 20),
        name="block",
    )(
        activations,
        norm_gain.reshape(1, channels),
        norm_bias.reshape(1, channels),
        conv_weight,
        cotangent.reshape(rows, width, n_out),
    )
    return (out.reshape((1,) + out.shape), weight_grad)


def solution(mesh):
    in_specs = (P("tm", "height", None, None), P(), P(), P(), P("tm", "height", None, None))
    out_specs = (P("tm", None, "height", None), P("height", None))
    return jax.shard_map(local, mesh=mesh, in_specs=in_specs, out_specs=out_specs, check_vma=False)
```

time: 318 us -> 55.4 us (0.17)
  waiting for transfers between devices: 155 us -> 0 us
  blocking collectives: 82.2 us -> 0 us
  Pallas kernels: 0 us -> 51.1 us
  matrix products: 35.4 us -> 0 us
  starting transfers between devices: 17.3 us -> 0 us
  between operations: 14.2 us -> 0.64 us
  other arithmetic: 9.63 us -> 0 us
    psum x1 -> x0, waiting for transfers between devices: 144 us -> none  [local(): summed = lax.psum(jnp.concatenate(blocks, axis=1), ('tm', 'height'))]
    psum x2 -> x0, blocking collectives: 82.2 us -> none  [the longest x1 42 us: local(): group_mean = lax.psum(local_sums, ('tm', 'height')) / entries]
    pallas_call x0 -> x1, Pallas kernels: none -> 51.1 us  [local(): pl.pallas_call(functools.partial(block_kernel, dims, factor), out_shape=(...]
    dot_general x18 -> x0, matrix products: 35.4 us -> none  [the longest x9 21.8 us: local(): jnp.einsum('frwk,kc->frcw', patches[tap_t:tap_t + frames, tap_r:tap_r + r...]
    ppermute x3 -> x0, waiting for transfers between devices: 11.1 us -> none  [the longest x1 10.2 us: shifted(): lax.ppermute(value, axis, [(source, source + steps) for source in range(f...]
    all_to_all x1 -> x0, starting transfers between devices: 8.75 us -> none  [local(): lax.all_to_all(conv_out, 'height', split_axis=2, concat_axis=1, tiled=True)]
    ppermute x3 -> x0, starting transfers between devices: 8.54 us -> none  [the longest x1 4.21 us: shifted(): lax.ppermute(value, axis, [(source, source + steps) for source in range(f...]
    convert_element_type x3 -> x0, other arithmetic: 4.01 us -> none  [the longest x1 1.59 us: local(): weight_grad = (own_grad * factor).astype(jnp.bfloat16)]
  transfers between devices with their start and end apart: 5 -> 0, of which waited for: 3 -> 0; matrix products, arithmetic and copies ran while one was open for 3% -> 0% of each run, Pallas kernels for 0% -> 0%
where the time goes in v2:
time: 55.4 us; the launch traced here: 55.1 us
  Pallas kernels  51.1 us (92%)
  local copies, waits for them, and re-layouts  3.42 us (6%)
  between operations  0.64 us (1%)
    pallas_call x1, Pallas kernels, local(): pl.pallas_call(functools.partial(block_kernel, dims, factor), out_shape=(...  51.1 us
    unnamed x2, local copies, waits for them, and re-layouts  3.42 us

profile of v2, /device:TPU:0, one launch (start us, length us, event | category | flops | bytes accessed | tf_op | source)
XLA Modules:
  0.0 55.1 jit_solution(9733845485150552054)
XLA Ops:
  0.6 51.1 %block.1 = (bf16[64,16,256]{2,1,0:T(8,128)(2,1)}, bf16[16,3456]{1,0:T(8,128)(2,1)}) custom-call(bf16[2,4,256,128]{3,2,1,0:T(8,128)(2,1)} %act.1, f32[1,128]{1,0:T(1,128)} %bitcast.6, f32[1,128]{1,0:T(1,128)} %bitcast.7, bf16[3456,256]{1,0:T(8,128)(2,1)} %weight_in.1, bf16[4,256,256]{2,1,0:T(8,128)(2,1)} %bitcast.4), custom_call_target="tpu_custom_call" | custom-call | tf_op jit(solution)/shard_map/block/pallas_call | solution.py:426
  51.7 1.9 %copy.9 = bf16[1,64,16,256]{3,2,1,0:T(8,128)(2,1)} copy(bf16[1,64,16,256]{3,2,1,0:T(8,128)(2,1)} %bitcast.5) | data formatting | bytes 1048576
  53.6 1.5 %copy.10 = bf16[16,3456]{1,0:T(8,128)(2,1)} copy(bf16[16,3456]{1,0:T(8,128)(2,1)} %get-tuple-element.9) | data formatting | bytes 221184

commit v3 on v2

--- a/solution.py
+++ b/solution.py
@@ -10,6 +10,7 @@
 
 GROUPS = 32
 KT = 3
+CUTS = 2
 MESH = pl.DeviceIdType.MESH
 ANY = pl.BlockSpec(memory_space=pl.ANY)
 VMEM = pl.BlockSpec(memory_space=pltpu.VMEM)
@@ -323,16 +324,16 @@
     arrived(1)
     start(6)
 
+    many = 2 if rows % 2 == 0 else 1
+
     def patch(t, y):
-        return [taps[t, pl.ds(pl.multiple_of((y + r) * width, width), width)] for r in range(KT)]
+        return [taps[t, pl.ds(pl.multiple_of((y * many + r) * width, width), many * width)] for r in range(KT)]
 
     def conv_own(y, carry):
         acc[y] = jnp.dot(jnp.concatenate(patch(2, y), axis=1), weight[2 * band :], preferred_element_type=F32)
         return carry
 
-    lax.fori_loop(0, rows, conv_own, 0)
-    early.start_second()
-
+    lax.fori_loop(0, rows // many, conv_own, 0)
     for index in (2, 5, 6):
         arrived(index)
 
@@ -348,14 +349,17 @@
         return carry
 
     lax.fori_loop(0, rows + 2, prepare_old, 0)
+    early.start_second()
 
     def conv_old(y, carry):
         lhs = jnp.concatenate(patch(0, y) + patch(1, y), axis=1)
         total = (acc[y] + jnp.dot(lhs, weight[0 : 2 * band], preferred_element_type=F32)) * 0.5
-        pooled[:, y] = total.T.astype(BF16).reshape(n_rows, own_rows, width)
-        return carry
-
-    lax.fori_loop(0, rows, conv_old, 0)
+        for k in range(many):
+            part = total[k * width : (k + 1) * width].T.astype(BF16)
+            pooled[:, y * many + k] = part.reshape(n_rows, own_rows, width)
+        return carry
+
+    lax.fori_loop(0, rows // many, conv_old, 0)
 
     def block(step, slot, other):
         return pltpu.make_async_remote_copy(
@@ -375,8 +379,8 @@
     out[pl.ds(height * rows, rows)] = pooled[height]
     early.start_third()
     late.start_second()
+    late.start_third()
     early.start_last(factor)
-    late.start_third()
     wgrad[:, 2 * band :] = early.finish()[:, :band]
     late.start_last(factor)
     wgrad[:, : 2 * band] = late.finish()[:, : 2 * band]
@@ -393,6 +397,22 @@
         return carry
 
     lax.fori_loop(1, n_dev, sent, 0)
+
+
+def deliver_kernel(block_in, grad_in, block_out, grad_out, block_mid, grad_mid, in_sem, out_sem):
+    size = block_in.shape[0] // CUTS
+    pieces = [tuple(r.at[pl.ds(i * size, size)] for r in (block_in, block_mid, block_out)) for i in range(CUTS)]
+    pieces.append((grad_in, grad_mid, grad_out))
+    arrivals, departures = [], []
+    for i, (source, middle, target) in enumerate(pieces):
+        arrivals.append(pltpu.make_async_copy(source, middle, in_sem.at[i]))
+        departures.append(pltpu.make_async_copy(middle, target, out_sem.at[i]))
+        arrivals[-1].start()
+    for arrival, departure in zip(arrivals, departures):
+        arrival.wait()
+        departure.start()
+    for departure in departures:
+        departure.wait()
 
 
 def local(activations, norm_gain, norm_bias, conv_weight, cotangent):
@@ -406,6 +426,8 @@
     dims = (n_time, n_rows, outer, inner)
     dma = pltpu.SemaphoreType.DMA
     factor = 0.5 / math.sqrt(frames * n_time * rows * n_rows * width)
+
+    many = 2 if rows % 2 == 0 else 1
 
     def stream(length):
         span = -(-length // (128 * n_time)) * 128
@@ -435,7 +457,7 @@
             pltpu.VMEM((2 * frames, rows + 2, width, channels), BF16),
             pltpu.VMEM((rows + 2, width, channels), BF16),
             pltpu.VMEM((KT, (rows + 2) * width, KT * channels), BF16),
-            pltpu.VMEM((rows, width, n_out), F32),
+            pltpu.VMEM((rows // many, many * width, n_out), F32),
             pltpu.VMEM((1, channels), F32),
             pltpu.VMEM((1, channels), F32),
             pltpu.VMEM((depth, n_out), BF16),
@@ -463,6 +485,23 @@
         conv_weight,
         cotangent.reshape(rows, width, n_out),
     )
+    out, weight_grad = pl.pallas_call(
+        deliver_kernel,
+        out_shape=(
+            jax.ShapeDtypeStruct(out.shape, BF16),
+            jax.ShapeDtypeStruct(weight_grad.shape, BF16),
+        ),
+        in_specs=[ANY] * 2,
+        out_specs=(ANY, ANY),
+        scratch_shapes=[
+            pltpu.VMEM(out.shape, BF16),
+            pltpu.VMEM(weight_grad.shape, BF16),
+            dma((CUTS + 1,)),
+            dma((CUTS + 1,)),
+        ],
+        compiler_params=pltpu.CompilerParams(vmem_limit_bytes=56 << 20),
+        name="deliver",
+    )(out, weight_grad)
     return (out.reshape((1,) + out.shape), weight_grad)
 
 

time: 55.4 us -> 51.2 us (0.924)
  local copies, waits for them, and re-layouts: 3.42 us -> 0 us
  Pallas kernels: 51.1 us -> 50.4 us
    unnamed x2 -> x0, local copies, waits for them, and re-layouts: 3.42 us -> none
    pallas_call x1, Pallas kernels: 51.1 us -> 48.6 us  [local(): pl.pallas_call(functools.partial(block_kernel, dims, factor), out_shape=(...]
    pallas_call x0 -> x1, Pallas kernels: none -> 1.82 us  [local(): pl.pallas_call(deliver_kernel, out_shape=(jax.ShapeDtypeStruct(out.shape,...]
where the time goes in v3:
time: 51.2 us; the launch traced here: 51.1 us
  Pallas kernels  50.4 us (98%)
  between operations  0.64 us (1%)
    pallas_call x1, Pallas kernels, local(): pl.pallas_call(functools.partial(block_kernel, dims, factor), out_shape=(...  48.6 us
    pallas_call x1, Pallas kernels, local(): pl.pallas_call(deliver_kernel, out_shape=(jax.ShapeDtypeStruct(out.shape,...  1.82 us

profile of v3, /device:TPU:0, one launch (start us, length us, event | category | flops | bytes accessed | tf_op | source)
XLA Modules:
  0.0 51.1 jit_solution(10772786393797571801)
XLA Ops:
  0.6 48.6 %block.1 = (bf16[64,16,256]{2,1,0:T(8,128)(2,1)}, bf16[16,3456]{1,0:T(8,128)(2,1)}) custom-call(bf16[2,4,256,128]{3,2,1,0:T(8,128)(2,1)} %act.1, f32[1,128]{1,0:T(1,128)} %bitcast.5, f32[1,128]{1,0:T(1,128)} %bitcast.6, bf16[3456,256]{1,0:T(8,128)(2,1)} %weight_in.1, bf16[4,256,256]{2,1,0:T(8,128)(2,1)} %bitcast.4), custom_call_target="tpu_custom_call" | custom-call | tf_op jit(solution)/shard_map/block/pallas_call | solution.py:448
  49.3 1.8 %deliver.1 = (bf16[64,16,256]{2,1,0:T(8,128)(2,1)}, bf16[16,3456]{1,0:T(8,128)(2,1)}) custom-call(bf16[64,16,256]{2,1,0:T(8,128)(2,1)} %get-tuple-element.6.block_in, bf16[16,3456]{1,0:T(8,128)(2,1)} %get-tuple-element.7.grad_in), custom_call_target="tpu_custom_call" | custom-call | tf_op jit(solution)/shard_map/deliver/pallas_call | solution.py:488
